TPU v7x, 32 devices: a whole 2x2x4 slice. The times are simulated.
32 devices in a mesh: row: 4 (over y, x), col: 8 (over z, core).
Axes of the slice: x: 2, y: 2, z: 4, core: 2. Of those that a mesh axis runs over, the one named last changes fastest.
Arguments:
- pointmaps: bfloat16 [64, 64, 2, 3, 14336], P('row', 'col'), may hold values from -6 to 6
- confidence: bfloat16 [64, 64, 2, 14336], P('row', 'col'), may hold values from 1 to 10
- valid_blocks: int32 [64, 64, 64], P('row', 'col'), may hold values 0 or 1
- log_depth: float32 [64, 14336], P('row', 'col'), may hold values from 0 to 1.4
- camera: float32 [64, 8], replicated, may hold values from -1 to 5.8, as said below
- pair_pose: float32 [64, 64, 8], P('row', 'col'), may hold values from -1 to 1.2, as said below
- step_sizes: float32 [3], replicated, may hold values from 0.02 to 0.2
Outputs:
- new_log_depth: float32 [64, 14336], P('row', 'col')
- new_camera: float32 [64, 8], replicated
- new_pair_pose: float32 [64, 64, 8], P('row', 'col')
Inputs may be any that keep to these rules, and one draw needn't show every extreme that they name: `camera`: columns 0 to 3 hold a quaternion whose first entry lies in 0.8 to 1.2 and the others in -0.3 to 0.3; columns 4 to 6 a translation in -1 to 1; column 7 a log focal length in pixels, 5.2 to 5.8. `pair_pose`: columns 0 to 3 hold a quaternion whose first entry lies in 0.8 to 1.2 and the others in -0.3 to 0.3; columns 4 to 6 a translation in -1 to 1; column 7 a log scale in -0.5 to 0.5.
All inputs are finite; a program needn't handle non-finite values. No bound on the sum of `valid_blocks` on one device may be relied on, other than what follows from the above.
Results may differ from a plain program's by a relative error of at most 0.00055.
Values sent between devices are 32-bit elements; how exact they have to be, the bound alone decides.
No kernel may reach another device: no remote copies, remote signals or barrier semaphores. Data moves between devices by JAX's collectives and lax.ppermute only.
A program may use at most 192 MiB of HBM per device.

v0:
```python
import jax
import jax.numpy as jnp
from jax import lax
from jax.sharding import PartitionSpec as P

IMAGES = 64
IMG_WIDTH = 224
IMG_HEIGHT = 224
WIN_ROWS = 64
ADAM_STEPS = 2
BETA_ONE = 0.9
BETA_TWO = 0.999
ADAM_EPS = 0.001
SOFTEN = 0.01


def rotation(quaternion):
    length = jnp.sqrt(jnp.sum(quaternion * quaternion, axis=-1))
    w = quaternion[..., 0] / length
    x = quaternion[..., 1] / length
    y = quaternion[..., 2] / length
    z = quaternion[..., 3] / length
    return [
        [1.0 - 2.0 * (y * y + z * z), 2.0 * (x * y - w * z), 2.0 * (x * z + w * y)],
        [2.0 * (x * y + w * z), 1.0 - 2.0 * (x * x + z * z), 2.0 * (y * z - w * x)],
        [2.0 * (x * z - w * y), 2.0 * (y * z + w * x), 1.0 - 2.0 * (x * x + y * y)],
    ]


def world_points(log_depths, cameras):
    pixel_count = log_depths.shape[-1]
    position = jnp.arange(pixel_count, dtype=jnp.int32)
    across = (position % IMG_WIDTH).astype(jnp.float32) - (IMG_WIDTH - 1) / 2.0
    downward = (position // IMG_WIDTH + (IMG_HEIGHT - WIN_ROWS) // 2).astype(jnp.float32) - (
        IMG_HEIGHT - 1
    ) / 2.0
    focal_len = jnp.exp(cameras[:, 7:8])
    depth_map = jnp.exp(log_depths)
    ray_parts = (
        across[None, :] / focal_len * depth_map,
        downward[None, :] / focal_len * depth_map,
        depth_map,
    )
    turned = rotation(cameras[:, 0:4])
    return [
        turned[k][0][:, None] * ray_parts[0]
        + turned[k][1][:, None] * ray_parts[1]
        + turned[k][2][:, None] * ray_parts[2]
        + cameras[:, 4 + k][:, None]
        for k in range(3)
    ]


def pair_loss(
    first_depth,
    second_depth,
    first_camera,
    second_camera,
    pair_params,
    pointmaps,
    confidence,
    valid_blocks,
    first_ids,
    second_ids,
):
    first_world = world_points(first_depth, first_camera)
    second_world = world_points(second_depth, second_camera)
    pair_rotation = rotation(pair_params[..., 0:4])
    pair_scale = jnp.exp(pair_params[..., 7])
    pair_keep = (first_ids[:, None] != second_ids[None, :]).astype(jnp.float32)
    pixel_keep = (
        jnp.repeat(valid_blocks.astype(jnp.float32), IMG_WIDTH, axis=2) * pair_keep[:, :, None]
    )
    loss_sum = jnp.zeros((), jnp.float32)
    for side_index in range(2):
        if side_index == 0:
            points_side = [first_world[k][:, None, :] for k in range(3)]
        else:
            points_side = [second_world[k][None, :, :] for k in range(3)]
        source = [pointmaps[:, :, side_index, k, :].astype(jnp.float32) for k in range(3)]
        squared = SOFTEN
        for k in range(3):
            aligned = (
                pair_scale[..., None]
                * (
                    pair_rotation[k][0][..., None] * source[0]
                    + pair_rotation[k][1][..., None] * source[1]
                    + pair_rotation[k][2][..., None] * source[2]
                )
                + pair_params[..., 4 + k][..., None]
            )
            residual = points_side[k] - aligned
            squared = squared + residual * residual
        weight = confidence[:, :, side_index, :].astype(jnp.float32) * pixel_keep
        loss_sum = loss_sum + jnp.sum(weight * jnp.sqrt(squared))
    return loss_sum / (2.0 * (IMAGES - 1))


def adam_step(param, grad, first, second, step_number, step_size):
    first = BETA_ONE * first + (1.0 - BETA_ONE) * grad
    second = BETA_TWO * second + (1.0 - BETA_TWO) * grad * grad
    update = (
        step_size
        * (first / (1.0 - BETA_ONE**step_number))
        / (jnp.sqrt(second / (1.0 - BETA_TWO**step_number)) + ADAM_EPS)
    )
    return (param - update, first, second)


def body(pointmaps, confidence, valid_blocks, log_depth, camera, pair_pose, step_sizes):
    row_count = pointmaps.shape[0]
    col_count = pointmaps.shape[1]
    row_index = lax.axis_index("row")
    col_index = lax.axis_index("col")
    first_ids = row_index * row_count + jnp.arange(row_count, dtype=jnp.int32)
    second_ids = col_index * col_count + jnp.arange(col_count, dtype=jnp.int32)

    def local_loss(row_depth, col_depth, cameras, pair_params):
        first_camera = lax.dynamic_slice_in_dim(cameras, row_index * row_count, row_count, 0)
        second_camera = lax.dynamic_slice_in_dim(cameras, col_index * col_count, col_count, 0)
        return pair_loss(
            row_depth,
            col_depth,
            first_camera,
            second_camera,
            pair_params,
            pointmaps,
            confidence,
            valid_blocks,
            first_ids,
            second_ids,
        )

    depth_now, camera_now, pair_now = (log_depth, camera, pair_pose)
    depth_first = jnp.zeros_like(log_depth)
    depth_second = jnp.zeros_like(log_depth)
    camera_first = jnp.zeros_like(camera)
    camera_second = jnp.zeros_like(camera)
    pair_first = jnp.zeros_like(pair_pose)
    pair_second = jnp.zeros_like(pair_pose)
    for step_number in range(1, ADAM_STEPS + 1):
        row_depth = lax.all_gather(depth_now, "col", axis=1, tiled=True)
        every_image = lax.all_gather(depth_now, "row", axis=0, tiled=True)
        col_depth = lax.all_to_all(every_image, "col", split_axis=0, concat_axis=1, tiled=True)
        row_grad, col_grad, cam_grad, pair_grad = jax.grad(local_loss, argnums=(0, 1, 2, 3))(
            row_depth, col_depth, camera_now, pair_now
        )
        returned = lax.all_to_all(col_grad, "col", split_axis=1, concat_axis=0, tiled=True)
        from_cols = lax.psum_scatter(returned, "row", scatter_dimension=0, tiled=True)
        depth_grad = lax.psum_scatter(row_grad, "col", scatter_dimension=1, tiled=True)
        depth_grad = depth_grad + from_cols
        cam_total = lax.psum(cam_grad, ("row", "col"))
        depth_now, depth_first, depth_second = adam_step(
            depth_now, depth_grad, depth_first, depth_second, step_number, step_sizes[0]
        )
        camera_now, camera_first, camera_second = adam_step(
            camera_now, cam_total, camera_first, camera_second, step_number, step_sizes[1]
        )
        pair_now, pair_first, pair_second = adam_step(
            pair_now, pair_grad, pair_first, pair_second, step_number, step_sizes[2]
        )
    return (depth_now, camera_now, pair_now)


def solution(mesh):
    in_specs = (
        P("row", "col", None, None, None),
        P("row", "col", None, None),
        P("row", "col", None),
        P("row", "col"),
        P(),
        P("row", "col", None),
        P(),
    )
    out_specs = (P("row", "col"), P(), P("row", "col", None))
    return jax.shard_map(body, mesh=mesh, in_specs=in_specs, out_specs=out_specs, check_vma=False)
```

profile of v0, /device:TPU:10, one launch (start us, length us, event | category | flops | bytes accessed | tf_op | source)
XLA Modules:
  0.0 630.6 jit_solution(9990873873530797576)
XLA Ops:
  7.2 10.4 %all_gather.13 = f32[64,1792]{1,0:T(8,128)} all-gather(f32[16,1792]{1,0:T(8,128)} %param.10), channel_id=1, replica_groups=mesh['row'=4,'col'=8] {'row'}, dimensions={0}, use_global_device_ids=true | all-gather | bytes 573440 | tf_op jit(solution)/shard_map/all_gather | solution.py:143
  17.6 5.3 all-to-all-start
  23.0 23.3 %all_gather.12 = f32[16,14336]{1,0:T(8,128)S(1)} all-gather(f32[16,1792]{1,0:T(8,128)} %param.10), channel_id=1, replica_groups=mesh['row'=4,'col'=8] {'col'}, dimensions={1}, use_global_device_ids=true | all-gather | bytes 1032192 | tf_op jit(solution)/shard_map/all_gather | solution.py:142
  48.8 60.3 %fusion.394 = (bf16[16,8,1,1,14336]{4,2,3,1,0:T(2,128)(2,1)}, bf16[16,8,1,1,14336]{4,2,3,1,0:T(2,128)(2,1)}, bf16[16,8,1,1,14336]{4,2,3,1,0:T(2,128)(2,1)}, bf16...) fusion(bf16[16,8,2,3,14336]{4,2,3,1,0:T(2,128)(2,1)} %param.7), kind=kLoop, calls=%fused_computation.1094 | loop fusion | bytes 44040192 | tf_op jit(solution)/shard_map/jvp()/slice | solution.py:80
  109.1 3.8 broadcast_in_dim.14
  113.0 9.5 %reshape.2729 = f32[16,8,14336]{2,1,0:T(8,128)} reshape(f32[16,8,64,224]{3,2,1,0:T(8,128)} %broadcast_in_dim.14) | data formatting | bytes 14680064 | tf_op jit(solution)/shard_map/jvp()/reshape | solution.py:72
  122.5 17.9 %fusion.395 = (bf16[16,8,1,14336]{3,2,1,0:T(2,128)(2,1)}, bf16[16,8,1,14336]{3,2,1,0:T(2,128)(2,1)}) fusion(bf16[16,8,2,14336]{3,2,1,0:T(2,128)(2,1)} %param.8), kind=kLoop, calls=%fused_computation.1095 | loop fusion | bytes 14680064 | tf_op jit(solution)/shard_map/jvp()/slice | solution.py:94
  143.4 25.0 %add_multiply_fusion.9 = (f32[16,8,14336]{2,1,0:T(8,128)}, f32[16,8,14336]{2,1,0:T(8,128)}, bf16[16,8,14336]{2,1,0:T(8,128)(2,1)S(1)}, bf16[16,8,14336]{2,1,0:T(8,128)(2,1)}, bf16[16,8,14336]{2,1,0:T(8,128)(2,1)}) fusion(f32[16,8]{1,0:T(8,128)S(1)} %copy.311, f32[16,14336]{1,0:T(8,128)} %get-tuple-element.230, f32[16,8]{1,0:T(8,128)S(1)} %copy.292, ...), kind=kLoop, calls=%fused_computation.145 | loop fusion | flops 75235328 | bytes 50469888 | tf_op jit(solution)/shard_map/transpose(jvp())/add_any | solution.py:93
  168.5 14.6 %add_multiply_fusion.10 = (f32[16,8,14336]{2,1,0:T(8,128)}, f32[16,8,14336]{2,1,0:T(8,128)}) fusion(f32[16,8,14336]{2,1,0:T(8,128)} %get-tuple-element.191, f32[16,8]{1,0:T(8,128)S(1)} %copy.316, f32[16,14336]{1,0:T(8,128)S(1)} %get-tuple-element.229, f32[16,8]{1,0:T(8,128)S(1)} %copy.292, bf16[16,8,14336]{2,1,0:T(8,128)(2,1)} %get-tuple-element.194, ...), kind=kLoop, calls=%fused_computation.146 | loop fusion | flops 42205184 | bytes 34869760 | tf_op jit(solution)/shard_map/transpose(jvp())/add_any | solution.py:93
  183.1 31.7 %multiply_reduce_fusion.8 = (f32[16,8]{1,0:T(8,128)S(1)}, f32[16,8]{1,0:T(8,128)S(1)}, f32[16,8]{1,0:T(8,128)S(1)}, f32[16,8]{1,0:T(8,128)S(1)}, f32[16,8]{1,0:T...) fusion(f32[16,8,14336]{2,1,0:T(8,128)} %get-tuple-element.219, ...), kind=kLoop, calls=%fused_computation.164 | loop fusion | flops 103905360 | bytes 35795648 | tf_op jit(solution)/shard_map/transpose(jvp())/reduce_sum | solution.py:84
  214.9 3.5 multiply_reduce_fusion.24
  226.6 24.6 %add_multiply_fusion.8 = (f32[16,8,14336]{2,1,0:T(8,128)}, f32[16,8,14336]{2,1,0:T(8,128)}, bf16[16,8,14336]{2,1,0:T(8,128)(2,1)S(1)}, bf16[16,8,14336]{2,1,0:T(8,128)(2,1)S(1)}, bf16[16,8,14336]{2,1,0:T(8,128)(2,1)S(1)}) fusion(f32[8,14336]{1,0:T(8,128)S(1)} %get-tuple-element.236, f32[16,8]{1,0:T(8,128)S(1)} %copy.305, f32[16,8]{1,0:T(8,128)S(1)} %copy.292, ...), kind=kLoop, calls=%fused_computation.144 | loop fusion | flops 75235328 | bytes 49093632 | tf_op jit(solution)/shard_map/transpose(jvp())/add_any | solution.py:93
  251.2 13.2 %add_multiply_fusion.6 = (f32[16,8,14336]{2,1,0:T(8,128)S(1)}, f32[16,8,14336]{2,1,0:T(8,128)}) fusion(f32[16,8,14336]{2,1,0:T(8,128)} %get-tuple-element.181, f32[8,14336]{1,0:T(8,128)S(1)} %get-tuple-element.235, f32[16,8]{1,0:T(8,128)S(1)} %copy.311, f32[16,8]{1,0:T(8,128)S(1)} %copy.292, bf16[16,8,14336]{2,1,0:T(8,128)(2,1)S(1)} %get-tuple-element.184, ...), kind=kLoop, calls=%fused_computation.142 | loop fusion | flops 42205184 | bytes 33952256 | tf_op jit(solution)/shard_map/transpose(jvp())/add_any | solution.py:93
  264.5 31.6 %multiply_reduce_fusion.10 = (f32[16,8]{1,0:T(8,128)S(1)}, f32[16,8]{1,0:T(8,128)S(1)}, f32[16,8]{1,0:T(8,128)S(1)}, f32[16,8]{1,0:T(8,128)S(1)}, f32[16,8]{1,0:...) fusion(f32[16,8,14336]{2,1,0:T(8,128)} %get-tuple-element.217, ...), kind=kLoop, calls=%fused_computation.166 | loop fusion | flops 104249448 | bytes 34419296 | tf_op jit(solution)/shard_map/transpose(jvp())/reduce_sum | solution.py:84
  299.5 41.0 %psum.14 = f32[64,8]{0,1:T(8,128)S(1)} all-reduce(f32[64,8]{0,1:T(8,128)S(1)} %add_any.2152), channel_id=1, replica_groups=mesh['row'=4,'col'=8] {'row','col'}, use_global_device_ids=true, to_apply=%region_39.40 | all-reduce | flops 512 | bytes 4096 | tf_op jit(solution)/shard_map/psum | solution.py:152
  341.1 4.1 all-to-all-start.1
  347.2 9.1 %all-to-all-done.1 = f32[8,8,1792]{2,0,1:T(8,128)S(1)} async-done(((f32[8,8,1792]{2,0,1:T(8,128)}), f32[8,8,1792]{2,0,1:T(8,128)S(1)}, u32[]{:S(2)}, u32[]{:S(2)}) %all-to-all-start.1) | async-done | bytes 458784 | tf_op jit(solution)/shard_map/all_to_all | solution.py:148
  358.8 23.6 %reduce-scatter.7.cloned.1.call-done = f32[16,1792]{1,0:T(8,128)} async-done(((f32[64,1792]{1,0:T(8,128)}), f32[16,1792]{1,0:T(8,128)}) %reduce-scatter.7.cloned.1.call-update) | async-done | bytes 114704 | tf_op jit(solution)/shard_map/reduce_scatter | solution.py:149
  384.4 9.5 %all_gather.15 = f32[64,1792]{1,0:T(8,128)} all-gather(f32[16,1792]{1,0:T(8,128)S(1)} %divide_subtract_fusion), channel_id=1, replica_groups=mesh['row'=4,'col'=8] {'row'}, dimensions={0}, use_global_device_ids=true | all-gather | bytes 573440 | tf_op jit(solution)/shard_map/all_gather | solution.py:143
  394.0 16.0 %all_gather.14 = f32[16,14336]{1,0:T(8,128)S(1)} all-gather(f32[16,1792]{1,0:T(8,128)S(1)} %divide_subtract_fusion), channel_id=1, replica_groups=mesh['row'=4,'col'=8] {'col'}, dimensions={1}, use_global_device_ids=true | all-gather | bytes 1032192 | tf_op jit(solution)/shard_map/all_gather | solution.py:142
  410.8 17.8 %add_multiply_fusion.3 = (f32[16,8,14336]{2,1,0:T(8,128)}, f32[16,8,14336]{2,1,0:T(8,128)}) fusion(f32[16,8]{1,0:T(8,128)S(1)} %copy.355, f32[16,14336]{1,0:T(8,128)S(1)} %get-tuple-element.227, f32[16,8]{1,0:T(8,128)S(1)} %copy.347, bf16[16,8,14336]{2,1,0:T(8,128)(2,1)} %get-tuple-element.194, f32[16,8]{1,0:T(8,128)S(1)} %copy.354, ...), kind=kLoop, calls=%fused_computation.139 | loop fusion | flops 75235328 | bytes 39459840 | tf_op jit(solution)/shard_map/transpose(jvp())/add_any | solution.py:93
  428.6 11.2 %add_multiply_fusion.4 = (f32[16,8,14336]{2,1,0:T(8,128)}, f32[16,8,14336]{2,1,0:T(8,128)}) fusion(f32[16,8,14336]{2,1,0:T(8,128)} %get-tuple-element.161, f32[16,8]{1,0:T(8,128)S(1)} %copy.359, f32[16,14336]{1,0:T(8,128)S(1)} %get-tuple-element.226, f32[16,8]{1,0:T(8,128)S(1)} %copy.347, bf16[16,8,14336]{2,1,0:T(8,128)(2,1)S(1)} %copy-done.6, ...), kind=kLoop, calls=%fused_computation.140 | loop fusion | flops 42205184 | bytes 34869760 | tf_op jit(solution)/shard_map/transpose(jvp())/add_any | solution.py:93
  439.8 31.5 %multiply_reduce_fusion.2 = (f32[16,8]{1,0:T(8,128)S(1)}, f32[16,8]{1,0:T(8,128)}, f32[16,8]{1,0:T(8,128)S(1)}, f32[16,8]{1,0:T(8,128)S(1)}, f32[16,8]{1,0:T(8,1...) fusion(f32[16,8,14336]{2,1,0:T(8,128)} %get-tuple-element.215, ...), kind=kLoop, calls=%fused_computation.150 | loop fusion | flops 103905360 | bytes 35795648 | tf_op jit(solution)/shard_map/transpose(jvp())/reduce_sum | solution.py:84
  471.4 2.9 multiply_reduce_fusion.13
  474.3 5.3 all-to-all-start.2
  486.3 4.4 all-to-all-done.2
  491.3 20.2 %add_multiply_fusion = (f32[16,8,14336]{2,1,0:T(8,128)}, f32[16,8,14336]{2,1,0:T(8,128)}) fusion(f32[8,14336]{1,0:T(8,128)S(1)} %get-tuple-element.234, f32[16,8]{1,0:T(8,128)S(1)} %copy.355, f32[16,8]{1,0:T(8,128)S(1)} %copy.347, bf16[16,8,14336]{2,1,0:T(8,128)(2,1)} %copy-done.11, f32[16,8]{1,0:T(8,128)S(1)} %copy.354, ...), kind=kLoop, calls=%fused_computation.136 | loop fusion | flops 75235328 | bytes 38083584 | tf_op jit(solution)/shard_map/transpose(jvp())/add_any | solution.py:93
  511.5 10.4 %add_multiply_fusion.2 = (f32[16,8,14336]{2,1,0:T(8,128)S(1)}, f32[16,8,14336]{2,1,0:T(8,128)}) fusion(f32[16,8,14336]{2,1,0:T(8,128)} %get-tuple-element.154, f32[8,14336]{1,0:T(8,128)S(1)} %get-tuple-element.233, f32[16,8]{1,0:T(8,128)S(1)} %copy.351, f32[16,8]{1,0:T(8,128)S(1)} %copy.347, bf16[16,8,14336]{2,1,0:T(8,128)(2,1)S(1)} %copy-done.12, ...), kind=kLoop, calls=%fused_computation.138 | loop fusion | flops 42205184 | bytes 33952256 | tf_op jit(solution)/shard_map/transpose(jvp())/add_any | solution.py:93
  521.9 32.2 %multiply_reduce_fusion.4 = (f32[16,8]{1,0:T(8,128)S(1)}, f32[16,8]{1,0:T(8,128)S(1)}, f32[16,8]{1,0:T(8,128)S(1)}, f32[16,8]{1,0:T(8,128)S(1)}, f32[16,8]{1,0:T...) fusion(f32[16,8,14336]{2,1,0:T(8,128)} %get-tuple-element.213, ...), kind=kLoop, calls=%fused_computation.152 | loop fusion | flops 104249448 | bytes 34419296 | tf_op jit(solution)/shard_map/transpose(jvp())/reduce_sum | solution.py:84
  557.7 6.3 all-to-all-start.3
  566.2 8.8 %all-to-all-done.3 = f32[8,8,1792]{2,0,1:T(8,128)S(1)} async-done(((f32[8,8,1792]{2,0,1:T(8,128)}), f32[8,8,1792]{2,0,1:T(8,128)S(1)}, u32[]{:S(2)}, u32[]{:S(2)}) %all-to-all-start.3) | async-done | bytes 458784 | tf_op jit(solution)/shard_map/all_to_all | solution.py:148
  579.1 42.3 %psum.15 = f32[64,8]{0,1:T(8,128)S(1)} all-reduce(f32[64,8]{0,1:T(8,128)S(1)} %add_any.2425), channel_id=1, replica_groups=mesh['row'=4,'col'=8] {'row','col'}, use_global_device_ids=true, to_apply=%region_109.110 | all-reduce | flops 512 | bytes 4096 | tf_op jit(solution)/shard_map/psum | solution.py:152
  (305 shorter events, 42.3 us)
Async XLA Ops:
  17.6 208.5 %all-to-all-start = ((f32[8,8,1792]{2,1,0:T(8,128)}), f32[8,8,1792]{2,1,0:T(8,128)S(1)}, u32[]{:S(2)}, u32[]{:S(2)}) async-start(f32[8,8,1792]{2,1,0:T(8,128)} %bitcast.39), calls=%async_computation.1 | async-start | bytes 917504 | tf_op jit(solution)/shard_map/all_to_all | solution.py:144
  22.9 335.9 %reduce-scatter.5.cloned.1.call-start = ((), (), s32[]{:S(2)}) async-start(), calls=%async_computation.8 | async-start | bytes 1032192 | tf_op jit(solution)/shard_map/reduce_scatter | solution.py:150
  47.1 93.9 %copy-start.26 = (f32[16,1]{0,1:T(1,128)}, f32[16,1]{0,1:T(1,128)S(1)}, u32[]{:S(2)}) copy-start(f32[16,1]{0,1:T(1,128)S(1)} %get-tuple-element.202) | copy-start | bytes 196
  47.1 94.6 %copy-start.39 = (f32[16]{0:T(128)}, f32[16]{0:T(128)S(1)}, u32[]{:S(2)}) copy-start(f32[16]{0:T(128)S(1)} %get-tuple-element.200) | copy-start | bytes 196
  48.8 60.3 %copy-start.19 = (s32[16,8,64]{2,1,0:T(8,128)S(1)}, s32[16,8,64]{2,1,0:T(8,128)}, u32[]{:S(2)}) copy-start(s32[16,8,64]{2,1,0:T(8,128)} %param.9) | copy-start | bytes 98308
  264.4 80.8 %copy-start.21 = (f32[16,8]{1,0:T(8,128)S(1)}, f32[16,8]{1,0:T(8,128)}, u32[]{:S(2)}) copy-start(f32[16,8]{1,0:T(8,128)} %get-tuple-element.62) | copy-start | bytes 1540
  264.4 82.0 %copy-start.18 = (f32[16,8,8]{0,2,1:T(8,128)S(1)}, f32[16,8,8]{0,2,1:T(8,128)}, u32[]{:S(2)}) copy-start(f32[16,8,8]{0,2,1:T(8,128)} %param.12) | copy-start | bytes 12292
  264.5 118.0 %copy-start.15 = (f32[16,1792]{1,0:T(8,128)S(1)}, f32[16,1792]{1,0:T(8,128)}, u32[]{:S(2)}) copy-start(f32[16,1792]{1,0:T(8,128)} %param.10) | copy-start | bytes 344068
  341.1 15.2 %all-to-all-start.1 = ((f32[8,8,1792]{2,0,1:T(8,128)}), f32[8,8,1792]{2,0,1:T(8,128)S(1)}, u32[]{:S(2)}, u32[]{:S(2)}) async-start(f32[8,8,1792]{2,0,1:T(8,128)} %get-tuple-element.225), calls=%async_computation.2 | async-start | bytes 917504 | tf_op jit(solution)/shard_map/all_to_all | solution.py:148
  345.3 37.2 %reduce-scatter.7.cloned.1.call-start = ((), (), s32[]{:S(2)}) async-start(), calls=%async_computation.9 | async-start | bytes 573440 | tf_op jit(solution)/shard_map/reduce_scatter | solution.py:149
  357.1 71.4 %copy-start.28 = (f32[8]{0:T(128)}, f32[8]{0:T(128)S(1)}, u32[]{:S(2)}) copy-start(f32[8]{0:T(128)S(1)} %multiply_reduce_fusion.48) | copy-start | bytes 100
  358.6 69.9 %copy-start.49 = (f32[8,1]{0,1:T(1,128)}, f32[8,1]{0,1:T(1,128)S(1)}, u32[]{:S(2)}) copy-start(f32[8,1]{0,1:T(1,128)S(1)} %get-tuple-element.310) | copy-start | bytes 100
  358.6 69.9 %copy-start.50 = (f32[8,1]{0,1:T(1,128)}, f32[8,1]{0,1:T(1,128)S(1)}, u32[]{:S(2)}) copy-start(f32[8,1]{0,1:T(1,128)S(1)} %get-tuple-element.311) | copy-start | bytes 100
  358.6 69.9 %copy-start.51 = (f32[8,1]{0,1:T(1,128)}, f32[8,1]{0,1:T(1,128)S(1)}, u32[]{:S(2)}) copy-start(f32[8,1]{0,1:T(1,128)S(1)} %get-tuple-element.312) | copy-start | bytes 100
  358.6 69.9 %copy-start.52 = (f32[8,1]{0,1:T(1,128)}, f32[8,1]{0,1:T(1,128)S(1)}, u32[]{:S(2)}) copy-start(f32[8,1]{0,1:T(1,128)S(1)} %get-tuple-element.313) | copy-start | bytes 100
  358.7 132.1 %copy-start.29 = (f32[8]{0:T(128)}, f32[8]{0:T(128)S(1)}, u32[]{:S(2)}) copy-start(f32[8]{0:T(128)S(1)} %get-tuple-element.308) | copy-start | bytes 100
  358.7 132.1 %copy-start.30 = (f32[8]{0:T(128)}, f32[8]{0:T(128)S(1)}, u32[]{:S(2)}) copy-start(f32[8]{0:T(128)S(1)} %get-tuple-element.309) | copy-start | bytes 100
  358.7 132.0 %copy-start.31 = (f32[8]{0:T(128)}, f32[8]{0:T(128)S(1)}, u32[]{:S(2)}) copy-start(f32[8]{0:T(128)S(1)} %get-tuple-element.332) | copy-start | bytes 100
  358.7 132.0 %copy-start.32 = (f32[8]{0:T(128)}, f32[8]{0:T(128)S(1)}, u32[]{:S(2)}) copy-start(f32[8]{0:T(128)S(1)} %get-tuple-element.333) | copy-start | bytes 100
  358.7 132.0 %copy-start.33 = (f32[8]{0:T(128)}, f32[8]{0:T(128)S(1)}, u32[]{:S(2)}) copy-start(f32[8]{0:T(128)S(1)} %get-tuple-element.334) | copy-start | bytes 100
  358.7 132.0 %copy-start.34 = (f32[8]{0:T(128)}, f32[8]{0:T(128)S(1)}, u32[]{:S(2)}) copy-start(f32[8]{0:T(128)S(1)} %get-tuple-element.335) | copy-start | bytes 100
  358.7 132.0 %copy-start.35 = (f32[8]{0:T(128)}, f32[8]{0:T(128)S(1)}, u32[]{:S(2)}) copy-start(f32[8]{0:T(128)S(1)} %get-tuple-element.336) | copy-start | bytes 100
  358.7 132.0 %copy-start.36 = (f32[8]{0:T(128)}, f32[8]{0:T(128)S(1)}, u32[]{:S(2)}) copy-start(f32[8]{0:T(128)S(1)} %get-tuple-element.352) | copy-start | bytes 100
  358.8 132.0 %copy-start.37 = (f32[8]{0:T(128)}, f32[8]{0:T(128)S(1)}, u32[]{:S(2)}) copy-start(f32[8]{0:T(128)S(1)} %get-tuple-element.353) | copy-start | bytes 100
  358.8 132.0 %copy-start.38 = (f32[8]{0:T(128)}, f32[8]{0:T(128)S(1)}, u32[]{:S(2)}) copy-start(f32[8]{0:T(128)S(1)} %get-tuple-element.354) | copy-start | bytes 100
  474.3 16.3 %all-to-all-start.2 = ((f32[8,8,1792]{2,1,0:T(8,128)}), f32[8,8,1792]{2,1,0:T(8,128)S(1)}, u32[]{:S(2)}, u32[]{:S(2)}) async-start(f32[8,8,1792]{2,1,0:T(8,128)} %bitcast.156), calls=%async_computation.5 | async-start | bytes 917504 | tf_op jit(solution)/shard_map/all_to_all | solution.py:144
  479.6 142.4 %reduce-scatter.9.cloned.1.call-start = ((), (), s32[]{:S(2)}) async-start(), calls=%async_computation.10 | async-start | bytes 1032192 | tf_op jit(solution)/shard_map/reduce_scatter | solution.py:150
  521.9 42.8 %copy-start.25 = (f32[16,8]{0,1:T(8,128)S(1)}, f32[16,8]{0,1:T(8,128)}, u32[]{:S(2)}) copy-start(f32[16,8]{0,1:T(8,128)} %copy.372) | copy-start | bytes 1540
  521.9 100.1 %copy-start.16 = (f32[16,1792]{1,0:T(8,128)S(1)}, f32[16,1792]{1,0:T(8,128)}, u32[]{:S(2)}) copy-start(f32[16,1792]{1,0:T(8,128)} %reduce-scatter.5.cloned.1.call-done) | copy-start | bytes 344068
  521.9 100.1 %copy-start.17 = (f32[16,1792]{1,0:T(8,128)S(1)}, f32[16,1792]{1,0:T(8,128)}, u32[]{:S(2)}) copy-start(f32[16,1792]{1,0:T(8,128)} %reduce-scatter.7.cloned.1.call-done) | copy-start | bytes 344068
  557.7 17.3 %all-to-all-start.3 = ((f32[8,8,1792]{2,0,1:T(8,128)}), f32[8,8,1792]{2,0,1:T(8,128)S(1)}, u32[]{:S(2)}, u32[]{:S(2)}) async-start(f32[8,8,1792]{2,0,1:T(8,128)} %get-tuple-element.224), calls=%async_computation.6 | async-start | bytes 917504 | tf_op jit(solution)/shard_map/all_to_all | solution.py:148
  563.9 58.1 %reduce-scatter.11.cloned.1.call-start = ((), (), s32[]{:S(2)}) async-start(), calls=%async_computation.11 | async-start | bytes 573440 | tf_op jit(solution)/shard_map/reduce_scatter | solution.py:149
  (37 other events, 845.2 us)
Sparse Core Ops, SparseCore 0:
  218.5 29.3 reduce-scatter.4
  357.2 25.1 reduce-scatter.6
  483.5 29.3 reduce-scatter.8
  575.9 26.0 reduce-scatter.10
where the time goes:
time: 641 us; the launch traced here: 631 us
  other arithmetic  297 us (46%)
  blocking collectives  143 us (22%)
  local copies, waits for them, and re-layouts  107 us (17%)
  waiting for transfers between devices  46 us (7%)
  starting transfers between devices  21 us (3%)
  between operations  17 us (3%)
    add_any x8, other arithmetic, pair_loss(): squared = squared + residual * residual  137 us
    reduce_sum x4, other arithmetic, pair_loss(): pair_scale[..., None]  127 us
    psum x2, blocking collectives, body(): cam_total = lax.psum(cam_grad, ('row', 'col'))  83.3 us
    slice x1, local copies, waits for them, and re-layouts, pair_loss(): pointmaps[:, :, side_index, k, :].astype(jnp.float32)  60.3 us
    all_gather x2, blocking collectives, body(): row_depth = lax.all_gather(depth_now, 'col', axis=1, tiled=True)  39.3 us
    reduce_scatter x2, waiting for transfers between devices, body(): lax.psum_scatter(returned, 'row', scatter_dimension=0, tiled=True)  23.6 us
    all_gather x2, blocking collectives, body(): every_image = lax.all_gather(depth_now, 'row', axis=0, tiled=True)  20 us
    slice x1, local copies, waits for them, and re-layouts, pair_loss(): weight = confidence[:, :, side_index, :].astype(jnp.float32) * pixel_keep  17.9 us
  transfers between devices with their start and end apart: 8, of which 4 were waited for; matrix products, arithmetic and copies ran while one was open for 53% of the time, Pallas kernels for 0%

commit v1 on v0

--- a/solution.py
+++ b/solution.py
@@ -149,7 +149,7 @@
         from_cols = lax.psum_scatter(returned, "row", scatter_dimension=0, tiled=True)
         depth_grad = lax.psum_scatter(row_grad, "col", scatter_dimension=1, tiled=True)
         depth_grad = depth_grad + from_cols
-        cam_total = lax.psum(cam_grad, ("row", "col"))
+        cam_total = lax.psum(lax.psum(cam_grad, "col"), "row")
         depth_now, depth_first, depth_second = adam_step(
             depth_now, depth_grad, depth_first, depth_second, step_number, step_sizes[0]
         )

time: 641 us -> 612 us (0.955)
  the two profiles are of different devices: /device:TPU:10 before, /device:TPU:0 now
where the time goes in v1:
time: 612 us; the launch traced here: 601 us
  other arithmetic  297 us (49%)
  blocking collectives  113 us (18%)
  local copies, waits for them, and re-layouts  107 us (17%)
  waiting for transfers between devices  51.2 us (8%)
  between operations  16.9 us (3%)
  starting transfers between devices  16.1 us (3%)
    add_any x8, other arithmetic, pair_loss(): squared = squared + residual * residual  137 us
    reduce_sum x4, other arithmetic, pair_loss(): pair_scale[..., None]  127 us
    slice x1, local copies, waits for them, and re-layouts, pair_loss(): pointmaps[:, :, side_index, k, :].astype(jnp.float32)  60.3 us
    psum x4, blocking collectives, body(): cam_total = lax.psum(lax.psum(cam_grad, 'col'), 'row')  49.6 us
    all_gather x2, blocking collectives, body(): row_depth = lax.all_gather(depth_now, 'col', axis=1, tiled=True)  40 us
    all_to_all x2, waiting for transfers between devices, body(): lax.all_to_all(col_grad, 'col', split_axis=1, concat_axis=0, tiled=True)  23.3 us
    all_gather x2, blocking collectives, body(): every_image = lax.all_gather(depth_now, 'row', axis=0, tiled=True)  23.3 us
    reduce_scatter x2, waiting for transfers between devices, body(): lax.psum_scatter(returned, 'row', scatter_dimension=0, tiled=True)  20.4 us
  transfers between devices with their start and end apart: 8, of which 4 were waited for; matrix products, arithmetic and copies ran while one was open for 55% of the time, Pallas kernels for 0%

profile of v1, /device:TPU:0, one launch (start us, length us, event | category | flops | bytes accessed | tf_op | source)
XLA Modules:
  0.0 601.3 jit_solution(2599728377569439690)
XLA Ops:
  7.2 12.9 %all_gather.13 = f32[64,1792]{1,0:T(8,128)} all-gather(f32[16,1792]{1,0:T(8,128)} %param.10), channel_id=1, replica_groups=mesh['row'=4,'col'=8] {'row'}, dimensions={0}, use_global_device_ids=true | all-gather | bytes 573440 | tf_op jit(solution)/shard_map/all_gather | solution.py:143
  20.1 4.9 all-to-all-start
  25.0 23.4 %all_gather.12 = f32[16,14336]{1,0:T(8,128)S(1)} all-gather(f32[16,1792]{1,0:T(8,128)} %param.10), channel_id=1, replica_groups=mesh['row'=4,'col'=8] {'col'}, dimensions={1}, use_global_device_ids=true | all-gather | bytes 1032192 | tf_op jit(solution)/shard_map/all_gather | solution.py:142
  51.0 60.3 %fusion.394 = (bf16[16,8,1,1,14336]{4,2,3,1,0:T(2,128)(2,1)}, bf16[16,8,1,1,14336]{4,2,3,1,0:T(2,128)(2,1)}, bf16[16,8,1,1,14336]{4,2,3,1,0:T(2,128)(2,1)}, bf16...) fusion(bf16[16,8,2,3,14336]{4,2,3,1,0:T(2,128)(2,1)} %param.7), kind=kLoop, calls=%fused_computation.1094 | loop fusion | bytes 44040192 | tf_op jit(solution)/shard_map/jvp()/slice | solution.py:80
  111.3 3.8 broadcast_in_dim.14
  115.2 9.5 %reshape.2729 = f32[16,8,14336]{2,1,0:T(8,128)} reshape(f32[16,8,64,224]{3,2,1,0:T(8,128)} %broadcast_in_dim.14) | data formatting | bytes 14680064 | tf_op jit(solution)/shard_map/jvp()/reshape | solution.py:72
  124.7 17.9 %fusion.395 = (bf16[16,8,1,14336]{3,2,1,0:T(2,128)(2,1)}, bf16[16,8,1,14336]{3,2,1,0:T(2,128)(2,1)}) fusion(bf16[16,8,2,14336]{3,2,1,0:T(2,128)(2,1)} %param.8), kind=kLoop, calls=%fused_computation.1095 | loop fusion | bytes 14680064 | tf_op jit(solution)/shard_map/jvp()/slice | solution.py:94
  145.5 25.0 %add_multiply_fusion.9 = (f32[16,8,14336]{2,1,0:T(8,128)}, f32[16,8,14336]{2,1,0:T(8,128)}, bf16[16,8,14336]{2,1,0:T(8,128)(2,1)S(1)}, bf16[16,8,14336]{2,1,0:T(8,128)(2,1)}, bf16[16,8,14336]{2,1,0:T(8,128)(2,1)}) fusion(f32[16,8]{1,0:T(8,128)S(1)} %copy.311, f32[16,14336]{1,0:T(8,128)} %get-tuple-element.230, f32[16,8]{1,0:T(8,128)S(1)} %copy.292, ...), kind=kLoop, calls=%fused_computation.145 | loop fusion | flops 75235328 | bytes 50469888 | tf_op jit(solution)/shard_map/transpose(jvp())/add_any | solution.py:93
  170.6 14.9 %add_multiply_fusion.10 = (f32[16,8,14336]{2,1,0:T(8,128)}, f32[16,8,14336]{2,1,0:T(8,128)}) fusion(f32[16,8,14336]{2,1,0:T(8,128)} %get-tuple-element.191, f32[16,8]{1,0:T(8,128)S(1)} %copy.316, f32[16,14336]{1,0:T(8,128)S(1)} %get-tuple-element.229, f32[16,8]{1,0:T(8,128)S(1)} %copy.292, bf16[16,8,14336]{2,1,0:T(8,128)(2,1)} %get-tuple-element.194, ...), kind=kLoop, calls=%fused_computation.146 | loop fusion | flops 42205184 | bytes 34869760 | tf_op jit(solution)/shard_map/transpose(jvp())/add_any | solution.py:93
  185.6 31.7 %multiply_reduce_fusion.8 = (f32[16,8]{1,0:T(8,128)S(1)}, f32[16,8]{1,0:T(8,128)S(1)}, f32[16,8]{1,0:T(8,128)S(1)}, f32[16,8]{1,0:T(8,128)S(1)}, f32[16,8]{1,0:T...) fusion(f32[16,8,14336]{2,1,0:T(8,128)} %get-tuple-element.219, ...), kind=kLoop, calls=%fused_computation.164 | loop fusion | flops 103905360 | bytes 35795648 | tf_op jit(solution)/shard_map/transpose(jvp())/reduce_sum | solution.py:84
  229.0 24.4 %add_multiply_fusion.8 = (f32[16,8,14336]{2,1,0:T(8,128)}, f32[16,8,14336]{2,1,0:T(8,128)}, bf16[16,8,14336]{2,1,0:T(8,128)(2,1)S(1)}, bf16[16,8,14336]{2,1,0:T(8,128)(2,1)S(1)}, bf16[16,8,14336]{2,1,0:T(8,128)(2,1)S(1)}) fusion(f32[8,14336]{1,0:T(8,128)S(1)} %get-tuple-element.236, f32[16,8]{1,0:T(8,128)S(1)} %copy.305, f32[16,8]{1,0:T(8,128)S(1)} %copy.292, ...), kind=kLoop, calls=%fused_computation.144 | loop fusion | flops 75235328 | bytes 49093632 | tf_op jit(solution)/shard_map/transpose(jvp())/add_any | solution.py:93
  253.4 13.2 %add_multiply_fusion.6 = (f32[16,8,14336]{2,1,0:T(8,128)S(1)}, f32[16,8,14336]{2,1,0:T(8,128)}) fusion(f32[16,8,14336]{2,1,0:T(8,128)} %get-tuple-element.181, f32[8,14336]{1,0:T(8,128)S(1)} %get-tuple-element.235, f32[16,8]{1,0:T(8,128)S(1)} %copy.311, f32[16,8]{1,0:T(8,128)S(1)} %copy.292, bf16[16,8,14336]{2,1,0:T(8,128)(2,1)S(1)} %get-tuple-element.184, ...), kind=kLoop, calls=%fused_computation.142 | loop fusion | flops 42205184 | bytes 33952256 | tf_op jit(solution)/shard_map/transpose(jvp())/add_any | solution.py:93
  266.7 31.6 %multiply_reduce_fusion.10 = (f32[16,8]{1,0:T(8,128)S(1)}, f32[16,8]{1,0:T(8,128)S(1)}, f32[16,8]{1,0:T(8,128)S(1)}, f32[16,8]{1,0:T(8,128)S(1)}, f32[16,8]{1,0:...) fusion(f32[16,8,14336]{2,1,0:T(8,128)} %get-tuple-element.217, ...), kind=kLoop, calls=%fused_computation.166 | loop fusion | flops 104249448 | bytes 34419296 | tf_op jit(solution)/shard_map/transpose(jvp())/reduce_sum | solution.py:84
  301.6 17.2 %psum.28 = f32[64,8]{0,1:T(8,128)S(1)} all-reduce(f32[64,8]{0,1:T(8,128)S(1)} %add_any.2152), channel_id=1, replica_groups=mesh['row'=4,'col'=8] {'col'}, use_global_device_ids=true, to_apply=%region_39.40 | all-reduce | flops 512 | bytes 4096 | tf_op jit(solution)/shard_map/psum | solution.py:152
  318.7 9.0 %psum.29 = f32[64,8]{0,1:T(8,128)S(1)} all-reduce(f32[64,8]{0,1:T(8,128)S(1)} %psum.28), channel_id=1, replica_groups=mesh['row'=4,'col'=8] {'row'}, use_global_device_ids=true, to_apply=%region_40.41 | all-reduce | flops 512 | bytes 4096 | tf_op jit(solution)/shard_map/psum | solution.py:152
  328.4 3.5 all-to-all-start.1
  333.9 11.8 %all-to-all-done.1 = f32[8,8,1792]{2,0,1:T(8,128)S(1)} async-done(((f32[8,8,1792]{2,0,1:T(8,128)}), f32[8,8,1792]{2,0,1:T(8,128)S(1)}, u32[]{:S(2)}, u32[]{:S(2)}) %all-to-all-start.1) | async-done | bytes 458784 | tf_op jit(solution)/shard_map/all_to_all | solution.py:148
  348.3 20.4 %reduce-scatter.7.cloned.1.call-done = f32[16,1792]{1,0:T(8,128)} async-done(((f32[64,1792]{1,0:T(8,128)}), f32[16,1792]{1,0:T(8,128)}) %reduce-scatter.7.cloned.1.call-update) | async-done | bytes 114704 | tf_op jit(solution)/shard_map/reduce_scatter | solution.py:149
  370.6 10.4 %all_gather.15 = f32[64,1792]{1,0:T(8,128)} all-gather(f32[16,1792]{1,0:T(8,128)S(1)} %divide_subtract_fusion), channel_id=1, replica_groups=mesh['row'=4,'col'=8] {'row'}, dimensions={0}, use_global_device_ids=true | all-gather | bytes 573440 | tf_op jit(solution)/shard_map/all_gather | solution.py:143
  381.0 16.6 %all_gather.14 = f32[16,14336]{1,0:T(8,128)S(1)} all-gather(f32[16,1792]{1,0:T(8,128)S(1)} %divide_subtract_fusion), channel_id=1, replica_groups=mesh['row'=4,'col'=8] {'col'}, dimensions={1}, use_global_device_ids=true | all-gather | bytes 1032192 | tf_op jit(solution)/shard_map/all_gather | solution.py:142
  398.5 18.1 %add_multiply_fusion.3 = (f32[16,8,14336]{2,1,0:T(8,128)}, f32[16,8,14336]{2,1,0:T(8,128)}) fusion(f32[16,8]{1,0:T(8,128)S(1)} %copy.355, f32[16,14336]{1,0:T(8,128)S(1)} %get-tuple-element.227, f32[16,8]{1,0:T(8,128)S(1)} %copy.347, bf16[16,8,14336]{2,1,0:T(8,128)(2,1)} %get-tuple-element.194, f32[16,8]{1,0:T(8,128)S(1)} %copy.354, ...), kind=kLoop, calls=%fused_computation.139 | loop fusion | flops 75235328 | bytes 39459840 | tf_op jit(solution)/shard_map/transpose(jvp())/add_any | solution.py:93
  416.6 11.2 %add_multiply_fusion.4 = (f32[16,8,14336]{2,1,0:T(8,128)}, f32[16,8,14336]{2,1,0:T(8,128)}) fusion(f32[16,8,14336]{2,1,0:T(8,128)} %get-tuple-element.161, f32[16,8]{1,0:T(8,128)S(1)} %copy.359, f32[16,14336]{1,0:T(8,128)S(1)} %get-tuple-element.226, f32[16,8]{1,0:T(8,128)S(1)} %copy.347, bf16[16,8,14336]{2,1,0:T(8,128)(2,1)S(1)} %copy-done.6, ...), kind=kLoop, calls=%fused_computation.140 | loop fusion | flops 42205184 | bytes 34869760 | tf_op jit(solution)/shard_map/transpose(jvp())/add_any | solution.py:93
  427.8 31.5 %multiply_reduce_fusion.2 = (f32[16,8]{1,0:T(8,128)S(1)}, f32[16,8]{1,0:T(8,128)}, f32[16,8]{1,0:T(8,128)S(1)}, f32[16,8]{1,0:T(8,128)S(1)}, f32[16,8]{1,0:T(8,1...) fusion(f32[16,8,14336]{2,1,0:T(8,128)} %get-tuple-element.215, ...), kind=kLoop, calls=%fused_computation.150 | loop fusion | flops 103905360 | bytes 35795648 | tf_op jit(solution)/shard_map/transpose(jvp())/reduce_sum | solution.py:84
  462.3 4.1 all-to-all-start.2
  473.1 7.4 %all-to-all-done.2 = f32[8,8,1792]{2,1,0:T(8,128)S(1)} async-done(((f32[8,8,1792]{2,1,0:T(8,128)}), f32[8,8,1792]{2,1,0:T(8,128)S(1)}, u32[]{:S(2)}, u32[]{:S(2)}) %all-to-all-start.2) | async-done | bytes 458784 | tf_op jit(solution)/shard_map/all_to_all | solution.py:144
  481.1 20.2 %add_multiply_fusion = (f32[16,8,14336]{2,1,0:T(8,128)}, f32[16,8,14336]{2,1,0:T(8,128)}) fusion(f32[8,14336]{1,0:T(8,128)S(1)} %get-tuple-element.234, f32[16,8]{1,0:T(8,128)S(1)} %copy.355, f32[16,8]{1,0:T(8,128)S(1)} %copy.347, bf16[16,8,14336]{2,1,0:T(8,128)(2,1)} %copy-done.11, f32[16,8]{1,0:T(8,128)S(1)} %copy.354, ...), kind=kLoop, calls=%fused_computation.136 | loop fusion | flops 75235328 | bytes 38083584 | tf_op jit(solution)/shard_map/transpose(jvp())/add_any | solution.py:93
  501.4 10.4 %add_multiply_fusion.2 = (f32[16,8,14336]{2,1,0:T(8,128)S(1)}, f32[16,8,14336]{2,1,0:T(8,128)}) fusion(f32[16,8,14336]{2,1,0:T(8,128)} %get-tuple-element.154, f32[8,14336]{1,0:T(8,128)S(1)} %get-tuple-element.233, f32[16,8]{1,0:T(8,128)S(1)} %copy.351, f32[16,8]{1,0:T(8,128)S(1)} %copy.347, bf16[16,8,14336]{2,1,0:T(8,128)(2,1)S(1)} %copy-done.12, ...), kind=kLoop, calls=%fused_computation.138 | loop fusion | flops 42205184 | bytes 33952256 | tf_op jit(solution)/shard_map/transpose(jvp())/add_any | solution.py:93
  511.8 32.2 %multiply_reduce_fusion.4 = (f32[16,8]{1,0:T(8,128)S(1)}, f32[16,8]{1,0:T(8,128)S(1)}, f32[16,8]{1,0:T(8,128)S(1)}, f32[16,8]{1,0:T(8,128)S(1)}, f32[16,8]{1,0:T...) fusion(f32[16,8,14336]{2,1,0:T(8,128)} %get-tuple-element.213, ...), kind=kLoop, calls=%fused_computation.152 | loop fusion | flops 104249448 | bytes 34419296 | tf_op jit(solution)/shard_map/transpose(jvp())/reduce_sum | solution.py:84
  547.5 3.5 all-to-all-start.3
  553.4 11.5 %all-to-all-done.3 = f32[8,8,1792]{2,0,1:T(8,128)S(1)} async-done(((f32[8,8,1792]{2,0,1:T(8,128)}), f32[8,8,1792]{2,0,1:T(8,128)S(1)}, u32[]{:S(2)}, u32[]{:S(2)}) %all-to-all-start.3) | async-done | bytes 458784 | tf_op jit(solution)/shard_map/all_to_all | solution.py:148
  568.8 14.6 %psum.30 = f32[64,8]{0,1:T(8,128)S(1)} all-reduce(f32[64,8]{0,1:T(8,128)S(1)} %add_any.2425), channel_id=1, replica_groups=mesh['row'=4,'col'=8] {'col'}, use_global_device_ids=true, to_apply=%region_110.111 | all-reduce | flops 512 | bytes 4096 | tf_op jit(solution)/shard_map/psum | solution.py:152
  583.4 8.8 %psum.31 = f32[64,8]{0,1:T(8,128)S(1)} all-reduce(f32[64,8]{0,1:T(8,128)S(1)} %psum.30), channel_id=1, replica_groups=mesh['row'=4,'col'=8] {'row'}, use_global_device_ids=true, to_apply=%region_111.112 | all-reduce | flops 512 | bytes 4096 | tf_op jit(solution)/shard_map/psum | solution.py:152
  (307 shorter events, 48.5 us)
Async XLA Ops:
  20.1 208.5 %all-to-all-start = ((f32[8,8,1792]{2,1,0:T(8,128)}), f32[8,8,1792]{2,1,0:T(8,128)S(1)}, u32[]{:S(2)}, u32[]{:S(2)}) async-start(f32[8,8,1792]{2,1,0:T(8,128)} %bitcast.39), calls=%async_computation.1 | async-start | bytes 917504 | tf_op jit(solution)/shard_map/all_to_all | solution.py:144
  24.9 323.3 %reduce-scatter.5.cloned.1.call-start = ((), (), s32[]{:S(2)}) async-start(), calls=%async_computation.8 | async-start | bytes 1032192 | tf_op jit(solution)/shard_map/reduce_scatter | solution.py:150
  49.2 93.9 %copy-start.26 = (f32[16,1]{0,1:T(1,128)}, f32[16,1]{0,1:T(1,128)S(1)}, u32[]{:S(2)}) copy-start(f32[16,1]{0,1:T(1,128)S(1)} %get-tuple-element.202) | copy-start | bytes 196
  49.2 94.6 %copy-start.39 = (f32[16]{0:T(128)}, f32[16]{0:T(128)S(1)}, u32[]{:S(2)}) copy-start(f32[16]{0:T(128)S(1)} %get-tuple-element.200) | copy-start | bytes 196
  51.0 60.3 %copy-start.19 = (s32[16,8,64]{2,1,0:T(8,128)S(1)}, s32[16,8,64]{2,1,0:T(8,128)}, u32[]{:S(2)}) copy-start(s32[16,8,64]{2,1,0:T(8,128)} %param.9) | copy-start | bytes 98308
  266.6 65.3 %copy-start.21 = (f32[16,8]{1,0:T(8,128)S(1)}, f32[16,8]{1,0:T(8,128)}, u32[]{:S(2)}) copy-start(f32[16,8]{1,0:T(8,128)} %get-tuple-element.62) | copy-start | bytes 1540
  266.7 66.5 %copy-start.18 = (f32[16,8,8]{0,2,1:T(8,128)S(1)}, f32[16,8,8]{0,2,1:T(8,128)}, u32[]{:S(2)}) copy-start(f32[16,8,8]{0,2,1:T(8,128)} %param.12) | copy-start | bytes 12292
  266.7 102.0 %copy-start.15 = (f32[16,1792]{1,0:T(8,128)S(1)}, f32[16,1792]{1,0:T(8,128)}, u32[]{:S(2)}) copy-start(f32[16,1792]{1,0:T(8,128)} %param.10) | copy-start | bytes 344068
  328.4 17.3 %all-to-all-start.1 = ((f32[8,8,1792]{2,0,1:T(8,128)}), f32[8,8,1792]{2,0,1:T(8,128)S(1)}, u32[]{:S(2)}, u32[]{:S(2)}) async-start(f32[8,8,1792]{2,0,1:T(8,128)} %get-tuple-element.225), calls=%async_computation.2 | async-start | bytes 917504 | tf_op jit(solution)/shard_map/all_to_all | solution.py:148
  331.9 36.7 %reduce-scatter.7.cloned.1.call-start = ((), (), s32[]{:S(2)}) async-start(), calls=%async_computation.9 | async-start | bytes 573440 | tf_op jit(solution)/shard_map/reduce_scatter | solution.py:149
  346.6 69.9 %copy-start.28 = (f32[8]{0:T(128)}, f32[8]{0:T(128)S(1)}, u32[]{:S(2)}) copy-start(f32[8]{0:T(128)S(1)} %multiply_reduce_fusion.48) | copy-start | bytes 100
  348.1 68.4 %copy-start.49 = (f32[8,1]{0,1:T(1,128)}, f32[8,1]{0,1:T(1,128)S(1)}, u32[]{:S(2)}) copy-start(f32[8,1]{0,1:T(1,128)S(1)} %get-tuple-element.310) | copy-start | bytes 100
  348.1 68.4 %copy-start.50 = (f32[8,1]{0,1:T(1,128)}, f32[8,1]{0,1:T(1,128)S(1)}, u32[]{:S(2)}) copy-start(f32[8,1]{0,1:T(1,128)S(1)} %get-tuple-element.311) | copy-start | bytes 100
  348.1 68.4 %copy-start.51 = (f32[8,1]{0,1:T(1,128)}, f32[8,1]{0,1:T(1,128)S(1)}, u32[]{:S(2)}) copy-start(f32[8,1]{0,1:T(1,128)S(1)} %get-tuple-element.312) | copy-start | bytes 100
  348.1 68.4 %copy-start.52 = (f32[8,1]{0,1:T(1,128)}, f32[8,1]{0,1:T(1,128)S(1)}, u32[]{:S(2)}) copy-start(f32[8,1]{0,1:T(1,128)S(1)} %get-tuple-element.313) | copy-start | bytes 100
  348.1 132.4 %copy-start.29 = (f32[8]{0:T(128)}, f32[8]{0:T(128)S(1)}, u32[]{:S(2)}) copy-start(f32[8]{0:T(128)S(1)} %get-tuple-element.308) | copy-start | bytes 100
  348.1 132.4 %copy-start.30 = (f32[8]{0:T(128)}, f32[8]{0:T(128)S(1)}, u32[]{:S(2)}) copy-start(f32[8]{0:T(128)S(1)} %get-tuple-element.309) | copy-start | bytes 100
  348.2 132.4 %copy-start.31 = (f32[8]{0:T(128)}, f32[8]{0:T(128)S(1)}, u32[]{:S(2)}) copy-start(f32[8]{0:T(128)S(1)} %get-tuple-element.332) | copy-start | bytes 100
  348.2 132.4 %copy-start.32 = (f32[8]{0:T(128)}, f32[8]{0:T(128)S(1)}, u32[]{:S(2)}) copy-start(f32[8]{0:T(128)S(1)} %get-tuple-element.333) | copy-start | bytes 100
  348.2 132.4 %copy-start.33 = (f32[8]{0:T(128)}, f32[8]{0:T(128)S(1)}, u32[]{:S(2)}) copy-start(f32[8]{0:T(128)S(1)} %get-tuple-element.334) | copy-start | bytes 100
  348.2 132.4 %copy-start.34 = (f32[8]{0:T(128)}, f32[8]{0:T(128)S(1)}, u32[]{:S(2)}) copy-start(f32[8]{0:T(128)S(1)} %get-tuple-element.335) | copy-start | bytes 100
  348.2 132.4 %copy-start.35 = (f32[8]{0:T(128)}, f32[8]{0:T(128)S(1)}, u32[]{:S(2)}) copy-start(f32[8]{0:T(128)S(1)} %get-tuple-element.336) | copy-start | bytes 100
  348.2 132.4 %copy-start.36 = (f32[8]{0:T(128)}, f32[8]{0:T(128)S(1)}, u32[]{:S(2)}) copy-start(f32[8]{0:T(128)S(1)} %get-tuple-element.352) | copy-start | bytes 100
  348.2 132.4 %copy-start.37 = (f32[8]{0:T(128)}, f32[8]{0:T(128)S(1)}, u32[]{:S(2)}) copy-start(f32[8]{0:T(128)S(1)} %get-tuple-element.353) | copy-start | bytes 100
  348.2 132.4 %copy-start.38 = (f32[8]{0:T(128)}, f32[8]{0:T(128)S(1)}, u32[]{:S(2)}) copy-start(f32[8]{0:T(128)S(1)} %get-tuple-element.354) | copy-start | bytes 100
  462.3 18.2 %all-to-all-start.2 = ((f32[8,8,1792]{2,1,0:T(8,128)}), f32[8,8,1792]{2,1,0:T(8,128)S(1)}, u32[]{:S(2)}, u32[]{:S(2)}) async-start(f32[8,8,1792]{2,1,0:T(8,128)} %bitcast.156), calls=%async_computation.5 | async-start | bytes 917504 | tf_op jit(solution)/shard_map/all_to_all | solution.py:144
  466.4 126.4 %reduce-scatter.9.cloned.1.call-start = ((), (), s32[]{:S(2)}) async-start(), calls=%async_computation.10 | async-start | bytes 1032192 | tf_op jit(solution)/shard_map/reduce_scatter | solution.py:150
  511.7 40.1 %copy-start.25 = (f32[16,8]{0,1:T(8,128)S(1)}, f32[16,8]{0,1:T(8,128)}, u32[]{:S(2)}) copy-start(f32[16,8]{0,1:T(8,128)} %copy.372) | copy-start | bytes 1540
  511.7 81.1 %copy-start.16 = (f32[16,1792]{1,0:T(8,128)S(1)}, f32[16,1792]{1,0:T(8,128)}, u32[]{:S(2)}) copy-start(f32[16,1792]{1,0:T(8,128)} %reduce-scatter.5.cloned.1.call-done) | copy-start | bytes 344068
  511.7 81.1 %copy-start.17 = (f32[16,1792]{1,0:T(8,128)S(1)}, f32[16,1792]{1,0:T(8,128)}, u32[]{:S(2)}) copy-start(f32[16,1792]{1,0:T(8,128)} %reduce-scatter.7.cloned.1.call-done) | copy-start | bytes 344068
  547.5 17.3 %all-to-all-start.3 = ((f32[8,8,1792]{2,0,1:T(8,128)}), f32[8,8,1792]{2,0,1:T(8,128)S(1)}, u32[]{:S(2)}, u32[]{:S(2)}) async-start(f32[8,8,1792]{2,0,1:T(8,128)} %get-tuple-element.224), calls=%async_computation.6 | async-start | bytes 917504 | tf_op jit(solution)/shard_map/all_to_all | solution.py:148
  551.0 41.8 %reduce-scatter.11.cloned.1.call-start = ((), (), s32[]{:S(2)}) async-start(), calls=%async_computation.11 | async-start | bytes 573440 | tf_op jit(solution)/shard_map/reduce_scatter | solution.py:149
  (37 other events, 845.2 us)
Sparse Core Ops, SparseCore 0:
  220.9 32.4 reduce-scatter.4
  346.7 21.8 reduce-scatter.6
  470.4 32.6 reduce-scatter.8
  565.8 22.6 reduce-scatter.10
